TPU v7x, 32 devices: a whole 2x2x4 slice. The times are simulated.
32 devices in a mesh: tm: 16 (over z, y, x), col: 2 (over core).
Axes of the slice: x: 2, y: 2, z: 4, core: 2. Of those that a mesh axis runs over, the one named last changes fastest.
Arguments:
- rhs: float32 [16, 1024, 256], P('tm', 'col'), may hold values from -6 to 6
- inverse_blocks: float32 [3, 16, 1024, 1024], P(None, 'tm', None, 'col'), may hold values from -2 to 3, as said below
- lower_coupling: float32 [3, 16, 1024, 1024], P(None, 'tm', None, 'col'), may hold values from -0.1875 to 0.1875
- upper_coupling: float32 [3, 16, 1024, 1024], P(None, 'tm', None, 'col'), may hold values from -0.1875 to 0.1875
- tile_pattern: int32 [3, 16, 2, 8, 8], P(None, 'tm', None, None, 'col'), may hold values from 0 to 1, as said below
- tip_coupling: float32 [3, 16, 64, 1024], P(None, 'tm', None, 'col'), may hold values from -0.046875 to 0.046875
- tip_rhs: float32 [64, 256], replicated, may hold values from -6 to 6
Outputs:
- reduced: float32 [16, 1024, 256], P('tm', 'col')
- tip_reduced: float32 [64, 256], replicated
Inputs may be any that keep to these rules, and one draw needn't show every extreme that they name: Every inverse_blocks[l, j] is symmetric. tile_pattern[l, j, k, r, c] is 1 exactly where |r - c| is at most a half-width w[l, j, k] of 1 to 4; both half-widths 1 and 4 occur.
All inputs are finite; a program needn't handle non-finite values.
Results may differ from a plain program's by a relative error of at most 0.0001.
Values sent between devices are 32-bit elements; how exact they have to be, the bound alone decides.
A program may use at most 64 MiB of HBM per device.

v0:
```python
import jax
import jax.numpy as jnp
from jax import lax
from jax.sharding import PartitionSpec as P


def passed_along(block, axis, distance):
    devices = range(lax.axis_size(axis))
    route = [((i - distance) % len(devices), i) for i in devices]
    return lax.ppermute(block, axis, route)


def local(rhs, inverse_blocks, lower_coupling, upper_coupling, tile_pattern, tip_coupling, tip_rhs):
    highest = lax.Precision.HIGHEST
    own_cols = inverse_blocks.shape[3]
    block_order = inverse_blocks.shape[2]
    tiles_here = tile_pattern.shape[4]
    tiles_all = tile_pattern.shape[3]
    tile_size = block_order // tiles_all
    level_count = inverse_blocks.shape[0]

    def apply_pattern(coupling, pattern):
        reshaped_rows = coupling.reshape(tiles_all, tile_size, tiles_here, tile_size)
        masked = reshaped_rows * pattern.astype(jnp.float32)[:, None, :, None]
        return masked.reshape(block_order, own_cols)

    present_rows = rhs[0]
    pending = jnp.zeros(tip_rhs.shape, jnp.float32)
    for level_number in range(level_count):
        stride = 2**level_number
        lower_masked = apply_pattern(
            lower_coupling[level_number, 0], tile_pattern[level_number, 0, 0]
        )
        upper_masked = apply_pattern(
            upper_coupling[level_number, 0], tile_pattern[level_number, 0, 1]
        )
        inverse = inverse_blocks[level_number, 0]

        def row_term(first_row, row_count, input_rows=present_rows, inverse_here=inverse):
            return jnp.dot(
                inverse_here, input_rows, precision=highest, preferred_element_type=jnp.float32
            )

        solved = lax.psum_scatter(
            row_term(jnp.int32(0), own_cols * lax.axis_size("col")),
            "col",
            scatter_dimension=0,
            tiled=True,
        )
        whole_solved = lax.all_gather(solved, "col", axis=0, tiled=True)
        down_term = jnp.dot(
            lower_masked.T, whole_solved, precision=highest, preferred_element_type=jnp.float32
        )
        up_term = jnp.dot(
            upper_masked.T, whole_solved, precision=highest, preferred_element_type=jnp.float32
        )
        from_above = passed_along(down_term, "tm", -stride)
        from_below = passed_along(up_term, "tm", stride)
        present_rows = present_rows - from_above - from_below
        arrow_part = jnp.dot(
            tip_coupling[level_number, 0],
            solved,
            precision=highest,
            preferred_element_type=jnp.float32,
        )
        pending = pending + arrow_part
    tip_total = tip_rhs - lax.psum(pending, ("tm", "col"))
    return (present_rows[None], tip_total)


def solution(mesh):
    return jax.shard_map(
        local,
        mesh=mesh,
        in_specs=(
            P("tm", "col", None),
            P(None, "tm", None, "col"),
            P(None, "tm", None, "col"),
            P(None, "tm", None, "col"),
            P(None, "tm", None, None, "col"),
            P(None, "tm", None, "col"),
            P(),
        ),
        out_specs=(P("tm", "col", None), P()),
        check_vma=False,
    )
```

profile of v0, /device:TPU:0, one launch (start us, length us, event | category | flops | bytes accessed | tf_op | source)
XLA Modules:
  0.0 308.7 jit_solution(16763351207113429849)
XLA Ops:
  7.2 0.0 reduce-scatter.4.cloned.1.call-start
  7.2 4.5 %fusion.21 = f32[1024,256]{1,0:T(8,128)} fusion(f32[3,1,1024,512]{3,2,1,0:T(8,128)} %param.8, f32[1,512,256]{2,1,0:T(8,128)} %param.7), kind=kOutput, calls=%fused_computation.27 | convolution fusion | flops 1610612736 | bytes 3670016 | tf_op jit(solution)/shard_map/dot_general | solution.py:40
  11.7 0.0 reduce-scatter.4.cloned.1.call-update
  11.7 0.0 all-gather.4.cloned.1.call-start
  11.8 11.2 %reduce-scatter.4.cloned.1.call-done = f32[512,256]{1,0:T(8,128)} async-done(((f32[1024,256]{1,0:T(8,128)}), f32[512,256]{1,0:T(8,128)}) %reduce-scatter.4.cloned.1.call-update) | async-done | bytes 524304 | tf_op jit(solution)/shard_map/reduce_scatter | solution.py:44
  23.0 0.0 all-gather.4.cloned.1.call-update
  23.0 0.0 reduce-scatter.6.cloned.1.call-start
  23.1 0.1 copy.9
  23.2 0.1 copy.10
  23.3 11.6 %all-gather.4.cloned.1.call-done = f32[1024,256]{1,0:T(8,128)} async-done(((f32[512,256]{1,0:T(8,128)}), f32[1024,256]{1,0:T(8,128)}) %all-gather.4.cloned.1.call-update) | async-done | bytes 1048592 | tf_op jit(solution)/shard_map/all_gather | solution.py:50
  34.8 0.3 mul.66
  35.2 0.9 copy-done
  36.0 5.1 %fusion.10 = f32[512,256]{1,0:T(8,128)S(1)} fusion(f32[1024,256]{1,0:T(8,128)S(1)} %copy-done, f32[128,8,4,128]{3,2,1,0:T(4,128)S(1)} %bitcast.121, f32[3,1,1024,512]{3,2,1,0:T(8,128)} %param.9), kind=kOutput, calls=%fused_computation.16 | convolution fusion | flops 1611137024 | bytes 5767168 | tf_op jit(solution)/shard_map/dot_general | solution.py:51
  41.1 5.5 %collective-permute-start = (f32[512,256]{1,0:T(8,128)S(1)}, f32[512,256]{1,0:T(8,128)S(1)}, u32[]{:S(2)}, u32[]{:S(2)}) collective-permute-start(f32[512,256]{1,0:T(8,128)S(1)} %fusion.10), channel_id=1, source_target_pairs={{2,0},{4,2},{6,4},{8,6},{10,8},{12,10},{14,12},{16,14},{18,16},{20... | collective-permute-start | bytes 1572872 | tf_op jit(solution)/shard_map/ppermute | solution.py:10
  46.6 0.3 mul.69
  46.9 0.0 copy-start.3
  46.9 5.1 %fusion.8 = f32[512,256]{1,0:T(8,128)S(1)} fusion(f32[1024,256]{1,0:T(8,128)S(1)} %copy-done, f32[128,8,4,128]{3,2,1,0:T(4,128)S(1)} %bitcast.118, f32[3,1,1024,512]{3,2,1,0:T(8,128)} %param.10), kind=kOutput, calls=%fused_computation.13 | convolution fusion | flops 1611137024 | bytes 5767168 | tf_op jit(solution)/shard_map/dot_general | solution.py:54
  52.0 0.2 collective-permute-start.1
  52.3 5.9 %collective-permute-done = f32[512,256]{1,0:T(8,128)S(1)} collective-permute-done((f32[512,256]{1,0:T(8,128)S(1)}, f32[512,256]{1,0:T(8,128)S(1)}, u32[]{:S(2)}, u32[]{:S(2)}) %collective-permute-start) | collective-permute-done | bytes 524320 | tf_op jit(solution)/shard_map/ppermute | solution.py:10
  58.2 11.5 %collective-permute-done.1 = f32[512,256]{1,0:T(8,128)S(1)} collective-permute-done((f32[512,256]{1,0:T(8,128)S(1)}, f32[512,256]{1,0:T(8,128)S(1)}, u32[]{:S(2)}, u32[]{:S(2)}) %collective-permute-start.1) | collective-permute-done | bytes 524320 | tf_op jit(solution)/shard_map/ppermute | solution.py:10
  69.7 0.1 fusion.41
  69.8 6.1 %fusion.33 = f32[1024,256]{0,1:T(8,128)} fusion(f32[512,256]{1,0:T(8,128)S(1)} %fusion.41, f32[3,1,1024,512]{3,2,1,0:T(8,128)} %param.8), kind=kOutput, calls=%fused_computation.39 | convolution fusion | flops 1610612736 | bytes 3670016 | tf_op jit(solution)/shard_map/dot_general | solution.py:40
  75.9 0.0 reduce-scatter.6.cloned.1.call-update
  76.0 0.0 all-gather.6.cloned.1.call-start
  76.0 9.1 %reduce-scatter.6.cloned.1.call-done = f32[512,256]{0,1:T(8,128)} async-done(((f32[1024,256]{0,1:T(8,128)}), f32[512,256]{0,1:T(8,128)}) %reduce-scatter.6.cloned.1.call-update) | async-done | bytes 524304 | tf_op jit(solution)/shard_map/reduce_scatter | solution.py:44
  85.2 0.0 all-gather.6.cloned.1.call-update
  85.2 0.0 reduce-scatter.8.cloned.1.call-start
  85.2 0.1 copy.11
  85.3 0.1 copy.12
  85.4 11.4 %all-gather.6.cloned.1.call-done = f32[1024,256]{0,1:T(8,128)} async-done(((f32[512,256]{0,1:T(8,128)}), f32[1024,256]{0,1:T(8,128)}) %all-gather.6.cloned.1.call-update) | async-done | bytes 1048592 | tf_op jit(solution)/shard_map/all_gather | solution.py:50
  96.8 0.3 mul.72
  97.1 0.9 copy-done.2
  98.0 5.0 %fusion.6 = f32[512,256]{1,0:T(8,128)S(1)} fusion(f32[1024,256]{0,1:T(8,128)S(1)} %copy-done.2, f32[128,8,4,128]{3,2,1,0:T(4,128)S(1)} %bitcast.122, f32[3,1,1024,512]{3,2,1,0:T(8,128)} %param.9), kind=kOutput, calls=%fused_computation.10 | convolution fusion | flops 1611137024 | bytes 5767168 | tf_op jit(solution)/shard_map/dot_general | solution.py:51
  103.1 4.6 %collective-permute-start.2 = (f32[512,256]{1,0:T(8,128)S(1)}, f32[512,256]{1,0:T(8,128)S(1)}, u32[]{:S(2)}, u32[]{:S(2)}) collective-permute-start(f32[512,256]{1,0:T(8,128)S(1)} %fusion.6), channel_id=1, source_target_pairs={{4,0},{6,2},{8,4},{10,6},{12,8},{14,10},{16,12},{18,14},{20,16},{2... | collective-permute-start | bytes 1572872 | tf_op jit(solution)/shard_map/ppermute | solution.py:10
  107.6 0.3 mul.75
  108.0 5.0 %fusion.4 = f32[512,256]{1,0:T(8,128)S(1)} fusion(f32[1024,256]{0,1:T(8,128)S(1)} %copy-done.2, f32[128,8,4,128]{3,2,1,0:T(4,128)S(1)} %bitcast.119, f32[3,1,1024,512]{3,2,1,0:T(8,128)} %param.10), kind=kOutput, calls=%fused_computation.7 | convolution fusion | flops 1611137024 | bytes 5767168 | tf_op jit(solution)/shard_map/dot_general | solution.py:54
  113.0 0.3 collective-permute-start.3
  113.3 6.0 %collective-permute-done.2 = f32[512,256]{1,0:T(8,128)S(1)} collective-permute-done((f32[512,256]{1,0:T(8,128)S(1)}, f32[512,256]{1,0:T(8,128)S(1)}, u32[]{:S(2)}, u32[]{:S(2)}) %collective-permute-start.2) | collective-permute-done | bytes 524320 | tf_op jit(solution)/shard_map/ppermute | solution.py:10
  119.3 10.6 %collective-permute-done.3 = f32[512,256]{1,0:T(8,128)S(1)} collective-permute-done((f32[512,256]{1,0:T(8,128)S(1)}, f32[512,256]{1,0:T(8,128)S(1)}, u32[]{:S(2)}, u32[]{:S(2)}) %collective-permute-start.3) | collective-permute-done | bytes 524320 | tf_op jit(solution)/shard_map/ppermute | solution.py:10
  129.8 6.1 %fusion.36 = f32[1024,256]{0,1:T(8,128)} fusion(f32[3,1,1024,512]{3,2,1,0:T(8,128)} %param.8, f32[512,256]{1,0:T(8,128)S(1)} %collective-permute-done.3, f32[512,256]{1,0:T(8,128)S(1)} %fusion.41, f32[512,256]{1,0:T(8,128)S(1)} %collective-permute-done.2), kind=kOutput, calls=%fused_computation.40 | convolution fusion | flops 1610874880 | bytes 4718592 | tf_op jit(solution)/shard_map/dot_general | solution.py:40
  136.0 0.0 reduce-scatter.8.cloned.1.call-update
  136.0 0.0 all-gather.8.cloned.1.call-start
  136.0 11.0 %reduce-scatter.8.cloned.1.call-done = f32[512,256]{0,1:T(8,128)} async-done(((f32[1024,256]{0,1:T(8,128)}), f32[512,256]{0,1:T(8,128)}) %reduce-scatter.8.cloned.1.call-update) | async-done | bytes 524304 | tf_op jit(solution)/shard_map/reduce_scatter | solution.py:44
  147.0 0.0 all-gather.8.cloned.1.call-update
  147.1 0.0 all-reduce.2.cloned.1.call-start
  147.1 0.1 copy.13
  147.2 0.1 copy.14
  147.3 11.4 %all-gather.8.cloned.1.call-done = f32[1024,256]{0,1:T(8,128)} async-done(((f32[512,256]{0,1:T(8,128)}), f32[1024,256]{0,1:T(8,128)}) %all-gather.8.cloned.1.call-update) | async-done | bytes 1048592 | tf_op jit(solution)/shard_map/all_gather | solution.py:50
  158.7 0.3 mul.78
  159.0 0.9 copy-done.1
  159.9 5.0 %fusion.2 = f32[512,256]{1,0:T(8,128)S(1)} fusion(f32[1024,256]{0,1:T(8,128)S(1)} %copy-done.1, f32[128,8,4,128]{3,2,1,0:T(4,128)S(1)} %bitcast.123, f32[3,1,1024,512]{3,2,1,0:T(8,128)} %param.9), kind=kOutput, calls=%fused_computation.4 | convolution fusion | flops 1611137024 | bytes 5767168 | tf_op jit(solution)/shard_map/dot_general | solution.py:51
  164.9 3.7 %collective-permute-start.4 = (f32[512,256]{1,0:T(8,128)S(1)}, f32[512,256]{1,0:T(8,128)S(1)}, u32[]{:S(2)}, u32[]{:S(2)}) collective-permute-start(f32[512,256]{1,0:T(8,128)S(1)} %fusion.2), channel_id=1, source_target_pairs={{8,0},{10,2},{12,4},{14,6},{16,8},{18,10},{20,12},{22,14},{24,16},... | collective-permute-start | bytes 1572872 | tf_op jit(solution)/shard_map/ppermute | solution.py:10
  168.6 0.3 mul.81
  168.9 0.0 copy-start.7
  169.0 6.0 %fusion = f32[512,256]{1,0:T(8,128)} fusion(f32[1024,256]{0,1:T(8,128)S(1)} %copy-done.1, f32[128,8,4,128]{3,2,1,0:T(4,128)S(1)} %bitcast.120, f32[3,1,1024,512]{3,2,1,0:T(8,128)} %param.10), kind=kOutput, calls=%fused_computation.1 | convolution fusion | flops 1611137024 | bytes 5767168 | tf_op jit(solution)/shard_map/dot_general | solution.py:54
  175.0 0.0 collective-permute-start.5
  175.0 0.4 fusion.44
  175.4 0.6 convolution_add_fusion.1
  176.0 1.2 fusion.39
  177.3 0.0 all-reduce.2.cloned.1.call-update
  177.3 122.2 %all-reduce.2.cloned.1.call-done = f32[64,256]{1,0:T(8,128)} async-done(((f32[64,256]{1,0:T(8,128)}), f32[64,256]{1,0:T(8,128)}) %all-reduce.2.cloned.1.call-update) | async-done | bytes 65552 | tf_op jit(solution)/shard_map/psum | solution.py:67
  299.4 1.5 sub.27
  300.9 0.0 collective-permute-done.4
  300.9 1.0 subtract_bitcast_fusion
  (17 shorter events, 0.0 us)
Async XLA Ops:
  7.2 15.9 %copy-start.9 = (s32[3,1,2,8,4]{3,4,2,1,0:T(4,128)S(1)}, s32[3,1,2,8,4]{3,4,2,1,0:T(4,128)}, u32[]{:S(2)}) copy-start(s32[3,1,2,8,4]{3,4,2,1,0:T(4,128)} %param.11) | copy-start | bytes 2308
  7.2 15.8 %reduce-scatter.4.cloned.1.call-start = ((), (), s32[]{:S(2)}) async-start(), calls=%async_computation.3 | async-start | bytes 1572864 | tf_op jit(solution)/shard_map/reduce_scatter | solution.py:44
  11.7 23.1 %all-gather.4.cloned.1.call-start = ((), (), s32[]{:S(2)}) async-start(), calls=%async_computation.4 | async-start | bytes 1572864 | tf_op jit(solution)/shard_map/all_gather | solution.py:50
  23.0 62.1 %reduce-scatter.6.cloned.1.call-start = ((), (), s32[]{:S(2)}) async-start(), calls=%async_computation.5 | async-start | bytes 1572864 | tf_op jit(solution)/shard_map/reduce_scatter | solution.py:44
  34.8 1.2 copy-start
  41.1 17.1 %collective-permute-start = (f32[512,256]{1,0:T(8,128)S(1)}, f32[512,256]{1,0:T(8,128)S(1)}, u32[]{:S(2)}, u32[]{:S(2)}) collective-permute-start(f32[512,256]{1,0:T(8,128)S(1)} %fusion.10), channel_id=1, source_target_pairs={{2,0},{4,2},{6,4},{8,6},{10,8},{12,10},{14,12},{16,14},{18,16},{20... | collective-permute-start | bytes 1572872 | tf_op jit(solution)/shard_map/ppermute | solution.py:10
  46.9 22.8 %copy-start.3 = (f32[1,512,256]{2,1,0:T(8,128)S(1)}, f32[1,512,256]{2,1,0:T(8,128)}, u32[]{:S(2)}) copy-start(f32[1,512,256]{2,1,0:T(8,128)} %param.7) | copy-start | bytes 1572868
  52.0 17.7 %collective-permute-start.1 = (f32[512,256]{1,0:T(8,128)S(1)}, f32[512,256]{1,0:T(8,128)S(1)}, u32[]{:S(2)}, u32[]{:S(2)}) collective-permute-start(f32[512,256]{1,0:T(8,128)S(1)} %fusion.8), channel_id=1, source_target_pairs={{30,0},{0,2},{2,4},{4,6},{6,8},{8,10},{10,12},{12,14},{14,16},{16,... | collective-permute-start | bytes 1572872 | tf_op jit(solution)/shard_map/ppermute | solution.py:10
  76.0 20.8 %all-gather.6.cloned.1.call-start = ((), (), s32[]{:S(2)}) async-start(), calls=%async_computation.6 | async-start | bytes 1572864 | tf_op jit(solution)/shard_map/all_gather | solution.py:50
  85.2 61.9 %reduce-scatter.8.cloned.1.call-start = ((), (), s32[]{:S(2)}) async-start(), calls=%async_computation.7 | async-start | bytes 1572864 | tf_op jit(solution)/shard_map/reduce_scatter | solution.py:44
  96.8 1.2 copy-start.2
  103.1 16.2 %collective-permute-start.2 = (f32[512,256]{1,0:T(8,128)S(1)}, f32[512,256]{1,0:T(8,128)S(1)}, u32[]{:S(2)}, u32[]{:S(2)}) collective-permute-start(f32[512,256]{1,0:T(8,128)S(1)} %fusion.6), channel_id=1, source_target_pairs={{4,0},{6,2},{8,4},{10,6},{12,8},{14,10},{16,12},{18,14},{20,16},{2... | collective-permute-start | bytes 1572872 | tf_op jit(solution)/shard_map/ppermute | solution.py:10
  113.0 16.8 %collective-permute-start.3 = (f32[512,256]{1,0:T(8,128)S(1)}, f32[512,256]{1,0:T(8,128)S(1)}, u32[]{:S(2)}, u32[]{:S(2)}) collective-permute-start(f32[512,256]{1,0:T(8,128)S(1)} %fusion.4), channel_id=1, source_target_pairs={{28,0},{30,2},{0,4},{2,6},{4,8},{6,10},{8,12},{10,14},{12,16},{14,... | collective-permute-start | bytes 1572872 | tf_op jit(solution)/shard_map/ppermute | solution.py:10
  136.0 22.7 %all-gather.8.cloned.1.call-start = ((), (), s32[]{:S(2)}) async-start(), calls=%async_computation.8 | async-start | bytes 1572864 | tf_op jit(solution)/shard_map/all_gather | solution.py:50
  147.1 152.4 %all-reduce.2.cloned.1.call-start = ((), (), s32[]{:S(2)}) async-start(), calls=%async_computation.9 | async-start | bytes 131072 | tf_op jit(solution)/shard_map/psum | solution.py:67
  158.7 1.2 copy-start.1
  164.9 136.0 %collective-permute-start.4 = (f32[512,256]{1,0:T(8,128)S(1)}, f32[512,256]{1,0:T(8,128)S(1)}, u32[]{:S(2)}, u32[]{:S(2)}) collective-permute-start(f32[512,256]{1,0:T(8,128)S(1)} %fusion.2), channel_id=1, source_target_pairs={{8,0},{10,2},{12,4},{14,6},{16,8},{18,10},{20,12},{22,14},{24,16},... | collective-permute-start | bytes 1572872 | tf_op jit(solution)/shard_map/ppermute | solution.py:10
  168.9 6.0 %copy-start.4 = (f32[512,256]{1,0:T(8,128)S(1)}, f32[512,256]{1,0:T(8,128)}, u32[]{:S(2)}) copy-start(f32[512,256]{1,0:T(8,128)} %reduce-scatter.4.cloned.1.call-done) | copy-start | bytes 1572868
  168.9 6.0 %copy-start.7 = (f32[3,1,64,512]{3,2,1,0:T(8,128)S(1)}, f32[3,1,64,512]{3,2,1,0:T(8,128)}, u32[]{:S(2)}) copy-start(f32[3,1,64,512]{3,2,1,0:T(8,128)} %param.12) | copy-start | bytes 1179652
  169.0 6.4 %copy-start.5 = (f32[512,256]{0,1:T(8,128)S(1)}, f32[512,256]{0,1:T(8,128)}, u32[]{:S(2)}) copy-start(f32[512,256]{0,1:T(8,128)} %reduce-scatter.6.cloned.1.call-done) | copy-start | bytes 1572868
  169.0 7.1 %copy-start.6 = (f32[512,256]{0,1:T(8,128)S(1)}, f32[512,256]{0,1:T(8,128)}, u32[]{:S(2)}) copy-start(f32[512,256]{0,1:T(8,128)} %reduce-scatter.8.cloned.1.call-done) | copy-start | bytes 1572868
  175.0 124.5 %copy-start.8 = (f32[64,256]{1,0:T(8,128)S(1)}, f32[64,256]{1,0:T(8,128)}, u32[]{:S(2)}) copy-start(f32[64,256]{1,0:T(8,128)} %param.13) | copy-start | bytes 196612
  175.0 126.0 %collective-permute-start.5 = (f32[512,256]{1,0:T(8,128)}, f32[512,256]{1,0:T(8,128)S(1)}, u32[]{:S(2)}, u32[]{:S(2)}) collective-permute-start(f32[512,256]{1,0:T(8,128)} %fusion), channel_id=1, source_target_pairs={{24,0},{26,2},{28,4},{30,6},{0,8},{2,10},{4,12},{6,14},{8,16},{10,... | collective-permute-start | bytes 1572872 | tf_op jit(solution)/shard_map/ppermute | solution.py:10
Sparse Core Ops, SparseCore 0:
  11.9 11.1 reduce-scatter.3
  24.5 10.2 all-gather.3
  76.1 9.0 reduce-scatter.5
  86.6 10.1 all-gather.5
  136.1 10.8 reduce-scatter.7
  148.4 10.1 all-gather.7
  177.4 121.9 all-reduce.1
where the time goes:
time: 310 us; the launch traced here: 309 us
  waiting for transfers between devices  222 us (72%)
  matrix products  50.3 us (16%)
  starting transfers between devices  14.5 us (5%)
  between operations  14.3 us (5%)
  local copies, waits for them, and re-layouts  5.17 us (2%)
    psum x1, waiting for transfers between devices, local(): tip_total = tip_rhs - lax.psum(pending, ('tm', 'col'))  122 us
    all_gather x3, waiting for transfers between devices, local(): whole_solved = lax.all_gather(solved, 'col', axis=0, tiled=True)  34.4 us
    ppermute x6, waiting for transfers between devices, passed_along(): return lax.ppermute(block, axis, route)  33.9 us
    reduce_scatter x3, waiting for transfers between devices, local(): lax.psum_scatter(row_term(jnp.int32(0), own_cols * lax.axis_size('col')),...  31.4 us
    dot_general x3, matrix products, row_term(): jnp.dot(inverse_here, input_rows, precision=highest, preferred_element_ty...  16.7 us
    dot_general x3, matrix products, local(): jnp.dot(upper_masked.T, whole_solved, precision=highest, preferred_elemen...  16.1 us
    dot_general x3, matrix products, local(): jnp.dot(lower_masked.T, whole_solved, precision=highest, preferred_elemen...  15.1 us
    ppermute x6, starting transfers between devices, passed_along(): return lax.ppermute(block, axis, route)  14.2 us
  transfers between devices with their start and end apart: 13, of which 11 were waited for; matrix products, arithmetic and copies ran while one was open for 7% of the time, Pallas kernels for 0%

commit v1 on v0

v1 whole, which is shorter than its diff:
```python
import functools

import jax
import jax.numpy as jnp
from jax import lax
from jax.experimental import pallas as pl
from jax.experimental.pallas import tpu as pltpu
from jax.sharding import PartitionSpec as P

MESH = pl.DeviceIdType.MESH
LANES = 128
ROWS = 8


def halves_of(x):
    high = x.astype(jnp.bfloat16)
    low = (x - high.astype(jnp.float32)).astype(jnp.bfloat16)
    return high, low


def product(stacked, high, w_high, w_low):
    rows = high.shape[0]
    both = jnp.dot(stacked, w_high, preferred_element_type=jnp.float32)
    return both[:rows] + both[rows:] + jnp.dot(high, w_low, preferred_element_type=jnp.float32)


def kernel(
    dims,
    rhs_hbm,
    inv_hbm,
    low_hbm,
    up_hbm,
    pattern,
    tip_c,
    tip_rhs,
    out,
    tip_out,
    rhs_v,
    raw,
    w_high,
    w_low,
    cur,
    sol,
    send,
    recv,
    tip_acc,
    tip_in,
    tip_sum,
    tip_all,
    in_sem,
    rhs_sem,
    cur_s,
    cur_r,
    sol_s,
    sol_r,
    row_s,
    row_r,
    tip_s1,
    tip_r1,
    tip_s2,
    tip_r2,
):
    levels, T, C, block, m, R, F, tiles_all, H = dims
    tiles_here = m * tiles_all // block
    tile = block // tiles_all
    part = R // H
    N = T * C
    row = lax.axis_index("tm")
    col = lax.axis_index("col")
    me = row * C + col
    groups = F // ROWS
    blocks = part // LANES
    G = groups * blocks * H

    sources = (inv_hbm, low_hbm, up_hbm)

    def load(level, kind):
        return pltpu.make_async_copy(
            sources[kind].at[level, 0], raw.at[level, kind], in_sem.at[level, kind]
        )

    rhs_copy = pltpu.make_async_copy(rhs_hbm.at[0], rhs_v, rhs_sem)
    rhs_copy.start()
    for level in range(levels):
        for kind in range(3):
            load(level, kind).start()

    barrier = pltpu.get_barrier_semaphore()

    @pl.loop(1, N)
    def _(k):
        other = lax.rem(me + k, N)
        pl.semaphore_signal(
            barrier,
            inc=1,
            device_id={"tm": other // C, "col": lax.rem(other, C)},
            device_id_type=MESH,
        )

    rhs_copy.wait()
    cur[0, col] = rhs_v[...].T

    def split(level, kind):
        load(level, kind).wait()

        @pl.loop(0, tiles_all)
        def _(r):
            rows = pl.ds(pl.multiple_of(r * tile, tile), tile)
            for c in range(tiles_here):
                cols = pl.ds(c * tile, tile)
                w = raw[level, kind, rows, cols]
                if kind:
                    at = ((level * 2 + kind - 1) * tiles_all + r) * tiles_here + c
                    w = w * pattern[at]
                high, low = halves_of(w)
                w_high[level, kind, rows, cols] = high
                w_low[level, kind, rows, cols] = low

    def rows_of(h):
        return pl.ds(h * part, part)

    def col_copy(buf, sems_s, sems_r, level, h, k, owner, target):
        return pltpu.make_async_remote_copy(
            src_ref=buf.at[level, owner, rows_of(h)],
            dst_ref=buf.at[level, owner, rows_of(h)],
            send_sem=sems_s.at[level, h, k - 1],
            recv_sem=sems_r.at[level, h, k - 1],
            device_id={"tm": row, "col": target},
            device_id_type=MESH,
        )

    def share(buf, sems_s, sems_r, level, h):
        for k in range(1, C):
            col_copy(buf, sems_s, sems_r, level, h, k, col, lax.rem(col + k, C)).start()

    def arrived(buf, sems_s, sems_r, level, h, k):
        owner = lax.rem(col + C - k, C)
        col_copy(buf, sems_s, sems_r, level, h, k, owner, owner).wait_recv()

    def row_copy(level, h, way):
        stride = 2**level
        target = lax.rem(row + (T - stride if way == 0 else stride), T)
        return pltpu.make_async_remote_copy(
            src_ref=send.at[level, way, rows_of(h)],
            dst_ref=recv.at[level, way, rows_of(h)],
            send_sem=row_s.at[level, h, way],
            recv_sem=row_r.at[level, h, way],
            device_id={"tm": target, "col": col},
            device_id_type=MESH,
        )

    def term(buf, level, h, k, kinds, totals):
        owner = lax.rem(col + C - k, C)
        high, low = halves_of(buf[level, owner, rows_of(h)])
        stacked = jnp.concatenate([high, low], axis=0)
        rows = pl.ds(pl.multiple_of(owner * m, m), m)
        results = []
        for kind, total in zip(kinds, totals):
            value = product(stacked, high, w_high[level, kind, rows], w_low[level, kind, rows])
            results.append(value if total is None else total + value)
        return results

    def owner_of(t):
        return (t * N) // G

    def tip_copy1(t):
        owner = owner_of(t)
        slot = lax.rem(me - owner + N, N) - 1
        return pltpu.make_async_remote_copy(
            src_ref=tip_acc.at[t],
            dst_ref=tip_in.at[slot],
            send_sem=tip_s1.at[t],
            recv_sem=tip_r1,
            device_id={"tm": owner // C, "col": lax.rem(owner, C)},
            device_id_type=MESH,
        )

    def tip_copy2(k, t):
        other = lax.rem(me + k, N)
        return pltpu.make_async_remote_copy(
            src_ref=tip_sum,
            dst_ref=tip_all.at[t],
            send_sem=tip_s2.at[k - 1],
            recv_sem=tip_r2.at[t],
            device_id={"tm": other // C, "col": lax.rem(other, C)},
            device_id_type=MESH,
        )

    def each_tile(action):
        @pl.loop(0, G)
        def _(t):
            @pl.when(owner_of(t) != me)
            def _():
                action(t)

    def each_owned(action):
        @pl.loop(0, G)
        def _(t):
            @pl.when(owner_of(t) == me)
            def _():
                action(t)

    def each_other(action):
        @pl.loop(1, N)
        def _(k):
            action(k)

    def add_tip(level, h):
        high, low = halves_of(sol[level, col, rows_of(h)])
        t_high, t_low = halves_of(tip_c[level, 0])
        nt = (((1,), (1,)), ((), ()))
        dot = functools.partial(lax.dot_general, preferred_element_type=jnp.float32)
        value = dot(t_high, high, nt) + dot(t_high, low, nt) + dot(t_low, high, nt)
        for b in range(blocks):
            piece = value[:, b * LANES : (b + 1) * LANES].reshape(groups, ROWS, LANES)
            at = pl.ds((h * blocks + b) * groups, groups)
            if level == 0:
                tip_acc[at] = piece
            else:
                tip_acc[at] = tip_acc[at] + piece

    def settled(level, h):
        row_copy(level, h, 0).wait_recv()
        row_copy(level, h, 1).wait_recv()
        return (
            cur[level, col, rows_of(h)] - recv[level, 0, rows_of(h)] - recv[level, 1, rows_of(h)]
        )

    pl.semaphore_wait(barrier, N - 1)
    for h in range(H):
        share(cur, cur_s, cur_r, 0, h)
    split(0, 0)

    for level in range(levels):
        for h in range(H):
            if level:
                cur[level, col, rows_of(h)] = settled(level - 1, h)
                share(cur, cur_s, cur_r, level, h)
            total = [None]
            for k in range(C):
                if k:
                    arrived(cur, cur_s, cur_r, level, h, k)
                total = term(cur, level, h, k, (0,), total)
            sol[level, col, rows_of(h)] = total[0]
            share(sol, sol_s, sol_r, level, h)
            add_tip(level, h)
            if level == levels - 1 and h == H - 1:
                each_tile(lambda t: tip_copy1(t).start())
            if level == 0 and h == 0:
                split(0, 1)
                split(0, 2)
            totals = [None, None]
            for k in range(C - 1):
                if k:
                    arrived(sol, sol_s, sol_r, level, h, k)
                totals = term(sol, level, h, k, (1, 2), totals)
            k = C - 1
            if k:
                arrived(sol, sol_s, sol_r, level, h, k)
            for way in range(2):
                send[level, way, rows_of(h)] = term(sol, level, h, k, (1 + way,), totals[way : way + 1])[0]
                row_copy(level, h, way).start()
        if level < levels - 1:
            for kind in range(3):
                split(level + 1, kind)

    def reduce_mine(t):
        pltpu.make_async_copy(tip_in, tip_in, tip_r1).wait()
        tip_sum[...] = tip_acc[t] + jnp.sum(tip_in[...], axis=0)
        tip_all[t] = tip_sum[...]
        each_other(lambda k: tip_copy2(k, t).start())

    each_owned(reduce_mine)
    for h in range(H):
        out[0, :, h * part : (h + 1) * part] = settled(levels - 1, h).T
    each_tile(lambda t: tip_copy2(1, t).wait_recv())
    for h in range(H):
        for b in range(blocks):
            at = h * blocks + b
            lanes = slice(at * LANES, (at + 1) * LANES)
            total = tip_all[at * groups : (at + 1) * groups].reshape(F, LANES)
            tip_out[:, lanes] = tip_rhs[:, lanes] - total

    for level in range(levels):
        for h in range(H):
            for k in range(1, C):
                target = lax.rem(col + k, C)
                col_copy(cur, cur_s, cur_r, level, h, k, col, target).wait_send()
                col_copy(sol, sol_s, sol_r, level, h, k, col, target).wait_send()
            for way in range(2):
                row_copy(level, h, way).wait_send()
    each_tile(lambda t: tip_copy1(t).wait_send())
    each_owned(lambda t: each_other(lambda k: tip_copy2(k, t).wait_send()))


HALVES = 2


def solution(mesh):
    T, C = mesh.shape["tm"], mesh.shape["col"]

    def local(rhs, inverse, lower, upper, tile_pattern, tip_coupling, tip_rhs):
        levels, _, block, m = inverse.shape
        R = rhs.shape[2]
        F = tip_rhs.shape[0]
        H = HALVES
        dims = (levels, T, C, block, m, R, F, tile_pattern.shape[3], H)
        N = T * C
        G = (F // ROWS) * (R // LANES)
        f32, b16 = jnp.float32, jnp.bfloat16
        dma = pltpu.SemaphoreType.DMA
        peers = max(C - 1, 1)
        anywhere = pl.BlockSpec(memory_space=pl.ANY)
        vmem = pl.BlockSpec(memory_space=pltpu.VMEM)
        return pl.pallas_call(
            functools.partial(kernel, dims),
            out_shape=(
                jax.ShapeDtypeStruct((1, m, R), f32),
                jax.ShapeDtypeStruct((F, R), f32),
            ),
            in_specs=[anywhere] * 4 + [pl.BlockSpec(memory_space=pltpu.SMEM), vmem, vmem],
            out_specs=(vmem, vmem),
            scratch_shapes=[
                pltpu.VMEM((m, R), f32),
                pltpu.VMEM((levels, 3, block, m), f32),
                pltpu.VMEM((levels, 3, block, m), b16),
                pltpu.VMEM((levels, 3, block, m), b16),
                pltpu.VMEM((levels, C, R, m), f32),
                pltpu.VMEM((levels, C, R, m), f32),
                pltpu.VMEM((levels, 2, R, m), f32),
                pltpu.VMEM((levels, 2, R, m), f32),
                pltpu.VMEM((G, ROWS, LANES), f32),
                pltpu.VMEM((N - 1, ROWS, LANES), f32),
                pltpu.VMEM((ROWS, LANES), f32),
                pltpu.VMEM((G, ROWS, LANES), f32),
                dma((levels, 3)),
                dma,
                dma((levels, H, peers)),
                dma((levels, H, peers)),
                dma((levels, H, peers)),
                dma((levels, H, peers)),
                dma((levels, H, 2)),
                dma((levels, H, 2)),
                dma((G,)),
                dma,
                dma((N - 1,)),
                dma((G,)),
            ],
            compiler_params=pltpu.CompilerParams(
                collective_id=0, has_side_effects=True, vmem_limit_bytes=60 * 2**20
            ),
        )(
            rhs,
            inverse,
            lower,
            upper,
            tile_pattern.astype(f32).reshape(-1),
            tip_coupling,
            tip_rhs,
        )

    return jax.shard_map(
        local,
        mesh=mesh,
        in_specs=(
            P("tm", "col", None),
            P(None, "tm", None, "col"),
            P(None, "tm", None, "col"),
            P(None, "tm", None, "col"),
            P(None, "tm", None, None, "col"),
            P(None, "tm", None, "col"),
            P(),
        ),
        out_specs=(P("tm", "col", None), P()),
        check_vma=False,
    )
```

time: 310 us -> 95.5 us (0.31)
  waiting for transfers between devices: 222 us -> 0 us
  Pallas kernels: 0 us -> 89.7 us
  matrix products: 50.3 us -> 0 us
  starting transfers between devices: 14.5 us -> 0 us
  between operations: 14.3 us -> 0.64 us
    psum x1 -> x0, waiting for transfers between devices: 122 us -> none  [local(): tip_total = tip_rhs - lax.psum(pending, ('tm', 'col'))]
    pallas_call x0 -> x1, Pallas kernels: none -> 89.7 us  [local(): pl.pallas_call(functools.partial(kernel, dims), out_shape=(jax.ShapeDtype...]
    dot_general x12 -> x0, matrix products: 50.3 us -> none  [the longest x3 16.7 us: row_term(): jnp.dot(inverse_here, input_rows, precision=highest, preferred_element_ty...]
    all_gather x3 -> x0, waiting for transfers between devices: 34.4 us -> none  [local(): whole_solved = lax.all_gather(solved, 'col', axis=0, tiled=True)]
    ppermute x6 -> x0, waiting for transfers between devices: 33.9 us -> none  [passed_along(): return lax.ppermute(block, axis, route)]
    reduce_scatter x3 -> x0, waiting for transfers between devices: 31.4 us -> none  [local(): lax.psum_scatter(row_term(jnp.int32(0), own_cols * lax.axis_size('col')),...]
    ppermute x6 -> x0, starting transfers between devices: 14.2 us -> none  [passed_along(): return lax.ppermute(block, axis, route)]
  transfers between devices with their start and end apart: 13 -> 0, of which waited for: 11 -> 0; matrix products, arithmetic and copies ran while one was open for 7% -> 0% of each run, Pallas kernels for 0% -> 0%
where the time goes in v1:
time: 95.5 us; the launch traced here: 95.2 us
  Pallas kernels  89.7 us (94%)
  local copies, waits for them, and re-layouts  4.12 us (4%)
    pallas_call x1, Pallas kernels, local(): pl.pallas_call(functools.partial(kernel, dims), out_shape=(jax.ShapeDtype...  89.7 us
    unnamed x2, local copies, waits for them, and re-layouts  3.34 us

profile of v1, /device:TPU:0, one launch (start us, length us, event | category | flops | bytes accessed | tf_op | source)
XLA Modules:
  0.0 95.2 jit_solution(4517671221223051690)
XLA Ops:
  0.6 0.7 convert_element_type.3
  1.3 0.1 copy.9
  1.5 0.7 reshape.7.pattern
  2.1 89.7 %shard_map.86 = (f32[1,512,256]{2,1,0:T(8,128)}, f32[64,256]{1,0:T(8,128)}) custom-call(f32[1,512,256]{2,1,0:T(8,128)} %rhs_hbm.1, f32[3,1,1024,512]{3,2,1,0:T(8,128)} %inv_hbm.1, f32[3,1,1024,512]{3,2,1,0:T(8,128)} %low_hbm.1, f32[3,1,1024,512]{3,2,1,0:T(8,128)} %up_hbm.1, f32[192]{0:T(256)} %reshape.7.pattern, f32[3,1,64,512]{3,2,1,0:T(8,128)} %tip_c.1, ...), custom_call_target="tpu_custom_call" | custom-call | tf_op jit(solution)/shard_map/pallas_call | solution.py:315
  91.8 1.9 %copy.12 = f32[1,512,256]{2,1,0:T(8,128)} copy(f32[1,512,256]{2,1,0:T(8,128)} %get-tuple-element.4) | data formatting | bytes 1048576
  93.7 1.5 %copy.13 = f32[64,256]{1,0:T(8,128)} copy(f32[64,256]{1,0:T(8,128)} %get-tuple-element.5) | data formatting | bytes 131072

commit v2 on v1

--- a/solution.py
+++ b/solution.py
@@ -43,6 +43,7 @@
     sol,
     send,
     recv,
+    joined,
     tip_acc,
     tip_in,
     tip_sum,
@@ -137,17 +138,35 @@
         owner = lax.rem(col + C - k, C)
         col_copy(buf, sems_s, sems_r, level, h, k, owner, owner).wait_recv()
 
+    def bit_of(level):
+        return lax.rem(row // 2**level, 2)
+
     def row_copy(level, h, way):
         stride = 2**level
-        target = lax.rem(row + (T - stride if way == 0 else stride), T)
+        if level == levels - 1:
+            target = lax.rem(row + (T - stride if way == 0 else stride), T)
+            source = send.at[level, way, rows_of(h)]
+        elif way == 0:
+            target = lax.rem(row + T - 2 * stride + 4 * stride * bit_of(level), T)
+            source = send.at[level, bit_of(level), rows_of(h)]
+        else:
+            target = row + stride - 2 * stride * bit_of(level)
+            source = joined.at[level, rows_of(h)]
         return pltpu.make_async_remote_copy(
-            src_ref=send.at[level, way, rows_of(h)],
+            src_ref=source,
             dst_ref=recv.at[level, way, rows_of(h)],
             send_sem=row_s.at[level, h, way],
             recv_sem=row_r.at[level, h, way],
             device_id={"tm": target, "col": col},
             device_id_type=MESH,
         )
+
+    def join(level, h):
+        row_copy(level, h, 0).wait_recv()
+        joined[level, rows_of(h)] = (
+            send[level, 1 - bit_of(level), rows_of(h)] + recv[level, 0, rows_of(h)]
+        )
+        row_copy(level, h, 1).start()
 
     def term(buf, level, h, k, kinds, totals):
         owner = lax.rem(col + C - k, C)
@@ -220,16 +239,18 @@
                 tip_acc[at] = tip_acc[at] + piece
 
     def settled(level, h):
-        row_copy(level, h, 0).wait_recv()
         row_copy(level, h, 1).wait_recv()
-        return (
-            cur[level, col, rows_of(h)] - recv[level, 0, rows_of(h)] - recv[level, 1, rows_of(h)]
-        )
-
+        value = cur[level, col, rows_of(h)] - recv[level, 1, rows_of(h)]
+        if level == levels - 1:
+            row_copy(level, h, 0).wait_recv()
+            value = value - recv[level, 0, rows_of(h)]
+        return value
+
+    for kind in range(3):
+        split(0, kind)
     pl.semaphore_wait(barrier, N - 1)
     for h in range(H):
         share(cur, cur_s, cur_r, 0, h)
-    split(0, 0)
 
     for level in range(levels):
         for h in range(H):
@@ -246,21 +267,27 @@
             add_tip(level, h)
             if level == levels - 1 and h == H - 1:
                 each_tile(lambda t: tip_copy1(t).start())
-            if level == 0 and h == 0:
-                split(0, 1)
-                split(0, 2)
+            if level < levels - 1:
+                ways = (bit_of(level), 1 - bit_of(level))
+            else:
+                ways = (0, 1)
+            kinds = (1 + ways[0], 1 + ways[1])
             totals = [None, None]
             for k in range(C - 1):
                 if k:
                     arrived(sol, sol_s, sol_r, level, h, k)
-                totals = term(sol, level, h, k, (1, 2), totals)
+                totals = term(sol, level, h, k, kinds, totals)
             k = C - 1
             if k:
                 arrived(sol, sol_s, sol_r, level, h, k)
-            for way in range(2):
-                send[level, way, rows_of(h)] = term(sol, level, h, k, (1 + way,), totals[way : way + 1])[0]
-                row_copy(level, h, way).start()
+            for i in range(2):
+                value = term(sol, level, h, k, kinds[i : i + 1], totals[i : i + 1])[0]
+                send[level, ways[i], rows_of(h)] = value
+                if i == 0 or level == levels - 1:
+                    row_copy(level, h, i).start()
         if level < levels - 1:
+            for h in range(H):
+                join(level, h)
             for kind in range(3):
                 split(level + 1, kind)
 
@@ -329,6 +356,7 @@
                 pltpu.VMEM((levels, C, R, m), f32),
                 pltpu.VMEM((levels, 2, R, m), f32),
                 pltpu.VMEM((levels, 2, R, m), f32),
+                pltpu.VMEM((max(levels - 1, 1), R, m), f32),
                 pltpu.VMEM((G, ROWS, LANES), f32),
                 pltpu.VMEM((N - 1, ROWS, LANES), f32),
                 pltpu.VMEM((ROWS, LANES), f32),

time: 95.5 us -> 89 us (0.932)
  Pallas kernels: 89.7 us -> 83.3 us
    pallas_call x1, Pallas kernels: 89.7 us -> 83.3 us  [local(): pl.pallas_call(functools.partial(kernel, dims), out_shape=(jax.ShapeDtype...]
where the time goes in v2:
time: 89 us; the launch traced here: 88.7 us
  Pallas kernels  83.3 us (94%)
  local copies, waits for them, and re-layouts  4.12 us (5%)
    pallas_call x1, Pallas kernels, local(): pl.pallas_call(functools.partial(kernel, dims), out_shape=(jax.ShapeDtype...  83.3 us
    unnamed x2, local copies, waits for them, and re-layouts  3.34 us

profile of v2, /device:TPU:0, one launch (start us, length us, event | category | flops | bytes accessed | tf_op | source)
XLA Modules:
  0.0 88.7 jit_solution(15461999242870809117)
XLA Ops:
  0.6 0.7 convert_element_type.3
  1.3 0.1 copy.9
  1.5 0.7 reshape.7.pattern
  2.1 83.3 %shard_map.86 = (f32[1,512,256]{2,1,0:T(8,128)}, f32[64,256]{1,0:T(8,128)}) custom-call(f32[1,512,256]{2,1,0:T(8,128)} %rhs_hbm.1, f32[3,1,1024,512]{3,2,1,0:T(8,128)} %inv_hbm.1, f32[3,1,1024,512]{3,2,1,0:T(8,128)} %low_hbm.1, f32[3,1,1024,512]{3,2,1,0:T(8,128)} %up_hbm.1, f32[192]{0:T(256)} %reshape.7.pattern, f32[3,1,64,512]{3,2,1,0:T(8,128)} %tip_c.1, ...), custom_call_target="tpu_custom_call" | custom-call | tf_op jit(solution)/shard_map/pallas_call | solution.py:342
  85.4 1.9 %copy.12 = f32[1,512,256]{2,1,0:T(8,128)} copy(f32[1,512,256]{2,1,0:T(8,128)} %get-tuple-element.4) | data formatting | bytes 1048576
  87.3 1.5 %copy.13 = f32[64,256]{1,0:T(8,128)} copy(f32[64,256]{1,0:T(8,128)} %get-tuple-element.5) | data formatting | bytes 131072
